TPU v7x, 512 devices: a whole 4x4x16 slice. The times are simulated.
512 devices in a mesh: pts: 16 (over z), elem: 32 (over y, x, core).
Axes of the slice: x: 4, y: 4, z: 16, core: 2. Of those that a mesh axis runs over, the one named last changes fastest.
Arguments:
- theta: float32 [1024, 1024], P('elem', 'pts'), may hold values from -3.140625 to 3.140625
- panel_rows: int32 [1024], P('elem'), may hold values from 0 to 1023, each once
- point_rows: int32 [32768], P('pts'), may hold values from 0 to 511
- point_cols: int32 [32768], P('pts'), may hold values from 0 to 255
- direct: float32 [2, 32768], P(None, 'pts'), may hold values from -3 to 3
- noise: float32 [32768], P('pts'), may hold values from 0.05 to 0.5
Outputs:
- phase_grad: float32 [1024, 1024], P('elem', 'pts')
- field: float32 [2, 32768], P(None, 'pts')
Inputs may be any that keep to these rules, and one draw needn't show every extreme that they name: `panel_rows`: each lattice row appears once.
All inputs are finite; a program needn't handle non-finite values.
Results may differ from a plain program's by a relative error of at most 0.0004.
Values sent between devices are 32-bit elements; how exact they have to be, the bound alone decides.
No kernel may reach another device: no remote copies, remote signals or barrier semaphores. Data moves between devices by JAX's collectives and lax.ppermute only.
A program may use at most 64 MiB of HBM per device.

v0:
```python
import math

import jax
import jax.numpy as jnp
from jax import lax
from jax.sharding import PartitionSpec as P

NX_EL = 1024
NY_EL = 1024


HIGH = lax.Precision.HIGHEST


def geometry(point_rows, point_cols):
    along_x = (point_rows.astype(jnp.float32) - 255.5) * 0.5
    along_y = (point_cols.astype(jnp.float32) - 127.5) * 0.5
    radius = jnp.sqrt(along_x * along_x + along_y * along_y + 1600.0)
    return (along_x / radius, along_y / radius, 80.0 / (radius * math.sqrt(NX_EL * NY_EL)))


def partial_field(slope_x, slope_y, lattice_x, lattice_y, phase_re, phase_im):
    beam_y = math.pi * slope_y[:, None] * lattice_y[None, :]
    left = jnp.concatenate([jnp.cos(beam_y), jnp.sin(beam_y)], 1)
    right = jnp.concatenate(
        [
            jnp.concatenate([phase_re.T, phase_im.T], 1),
            jnp.concatenate([-phase_im.T, phase_re.T], 1),
        ],
        0,
    )
    inner = jnp.dot(left, right, precision=HIGH, preferred_element_type=jnp.float32)
    width = phase_re.shape[0]
    inner_re = inner[:, :width]
    inner_im = inner[:, width:]
    beam_x = math.pi * slope_x[:, None] * lattice_x[None, :]
    cos_x = jnp.cos(beam_x)
    sin_x = jnp.sin(beam_x)
    return jnp.stack(
        [
            jnp.sum(cos_x * inner_re - sin_x * inner_im, 1),
            jnp.sum(cos_x * inner_im + sin_x * inner_re, 1),
        ]
    )


def surface_terms(slope_x, slope_y, q_re, q_im, lattice_x, lattice_y):
    beam_x = math.pi * slope_x[:, None] * lattice_x[None, :]
    cos_x = jnp.cos(beam_x)
    sin_x = jnp.sin(beam_x)
    weight_re = q_re[:, None] * cos_x - q_im[:, None] * sin_x
    weight_im = q_re[:, None] * sin_x + q_im[:, None] * cos_x
    beam_y = math.pi * slope_y[:, None] * lattice_y[None, :]
    left = jnp.concatenate([jnp.cos(beam_y), jnp.sin(beam_y)], 1)
    right = jnp.concatenate([weight_re, weight_im], 1)
    prod = lax.dot_general(
        left, right, (((0,), (0,)), ((), ())), precision=HIGH, preferred_element_type=jnp.float32
    )
    rows_y = lattice_y.shape[0]
    cols_x = lattice_x.shape[0]
    sum_re = prod[:rows_y, :cols_x] - prod[rows_y:, cols_x:]
    sum_im = prod[:rows_y, cols_x:] + prod[rows_y:, :cols_x]
    return jnp.concatenate([sum_re, sum_im], 1)


def block_size(points, cols_y):
    return math.gcd(points, min(points, max(256, 524288 // cols_y)))


def field_blocks(slope_x, slope_y, lattice_x, lattice_y, phase_re, phase_im):
    block = block_size(slope_x.shape[0], lattice_y.shape[0])
    count = slope_x.shape[0] // block

    def one_block(pair):
        return partial_field(pair[0], pair[1], lattice_x, lattice_y, phase_re, phase_im)

    parts = lax.map(one_block, (slope_x.reshape(count, block), slope_y.reshape(count, block)))
    return jnp.transpose(parts, (1, 0, 2)).reshape(2, count * block)


def terms_blocks(slope_x, slope_y, q_re, q_im, lattice_x, lattice_y):
    block = block_size(slope_x.shape[0], lattice_y.shape[0])
    count = slope_x.shape[0] // block
    start = jnp.zeros((lattice_y.shape[0], 2 * lattice_x.shape[0]), jnp.float32)

    def step(carry, items):
        return (
            carry + surface_terms(items[0], items[1], items[2], items[3], lattice_x, lattice_y),
            None,
        )

    items = (
        slope_x.reshape(count, block),
        slope_y.reshape(count, block),
        q_re.reshape(count, block),
        q_im.reshape(count, block),
    )
    total, unused = lax.scan(step, start, items)
    return total


def weights(field, scale, noise):
    power = noise + field[0] * field[0] + field[1] * field[1]
    return (field[0] * scale / power, -field[1] * scale / power)


def gradient(terms, phase_re, phase_im):
    cols_x = phase_re.shape[0]
    sum_re = terms[:, :cols_x].T
    sum_im = terms[:, cols_x:].T
    return -2.0 * (phase_re * sum_im + phase_im * sum_re)


def shards(theta, panel_rows, point_rows, point_cols, direct, noise):
    slope_x, slope_y, scale = geometry(point_rows, point_cols)
    phase_re = jnp.cos(theta)
    phase_im = jnp.sin(theta)
    lattice_x = panel_rows.astype(jnp.float32) - (NX_EL - 1) / 2.0
    cols_dev = theta.shape[1]
    phasors = jnp.stack([phase_re, phase_im])
    whole = lax.all_gather(phasors, "pts", axis=2, tiled=True)
    lattice_y = jnp.arange(NY_EL).astype(jnp.float32) - (NY_EL - 1) / 2.0
    partial_value = field_blocks(slope_x, slope_y, lattice_x, lattice_y, whole[0], whole[1])
    total = lax.psum(partial_value, "elem")
    field = direct + scale[None, :] * total
    q_re, q_im = weights(field, scale, noise)
    cols_here = jnp.arange(cols_dev * lax.axis_size("pts")).astype(jnp.float32) - (NY_EL - 1) / 2.0
    terms = lax.psum_scatter(
        terms_blocks(slope_x, slope_y, q_re, q_im, lattice_x, cols_here),
        "pts",
        scatter_dimension=0,
        tiled=True,
    )
    return (gradient(terms, phase_re, phase_im), field)


def solution(mesh):
    in_specs = (P("elem", "pts"), P("elem"), P("pts"), P("pts"), P(None, "pts"), P("pts"))
    out_specs = (P("elem", "pts"), P(None, "pts"))
    return jax.shard_map(shards, mesh=mesh, in_specs=in_specs, out_specs=out_specs, check_vma=False)
```

profile of v0, /device:TPU:2, one launch (start us, length us, event | category | flops | bytes accessed | tf_op | source)
XLA Modules:
  0.0 337.5 jit_solution(4195258781509086454)
XLA Ops:
  7.2 0.0 reduce-scatter.4.cloned.1.call-start
  7.2 0.8 copy.18
  8.0 0.1 fusion.39
  8.2 0.1 pad_maximum_fusion
  8.2 0.0 copy-start.2
  8.3 0.0 copy-start.3
  8.3 0.0 copy-start.5
  8.3 41.7 %all_gather.3 = f32[2,32,1024]{1,0,2:T(2,128)S(1)} all-gather(f32[2,32,64]{1,0,2:T(2,128)S(1)} %pad_maximum_fusion), channel_id=1, replica_groups=mesh['pts'=16,'elem'=32] {'pts'}, dimensions={2}, use_global_device_ids=true | all-gather | bytes 278528 | tf_op jit(solution)/shard_map/all_gather | solution.py:121
  49.9 0.8 fusion.38
  50.8 0.0 copy-done.2
  50.8 0.0 copy-done.3
  50.9 0.0 copy-done.5
  50.9 0.3 maximum_maximum_fusion
  51.2 0.0 copy-start.1
  51.3 0.0 copy-start.4
  51.3 47.9 %while.24 = (s32[]{:T(128)}, f32[4,2,512]{2,1,0:T(2,128)S(1)}, f32[4,512]{1,0:T(4,128)S(1)}, f32[32]{0:T(128)S(1)}, f32[4,512]{1,0:T(4,128)S(1)}, /*index=5*/f32[2048,64]{1,0:T(8,128)S(1)}, s32[]{:T(128)}) while((s32[]{:T(128)}, f32[4,2,512]{2,1,0:T(2,128)S(1)}, f32[4,512]{1,0:T(4,128)S(1)}, f32[32]{0:T(128)S(1)}, ...), condition=%wide.region_3.4_spmd.clone, body=%wide.region_0.3_spmd.clone.sunk | while | flops 807029760 | bytes 9208021 | solution.py:77
  51.3 7.3 %multiply_cosine_fusion.6 = (f32[512,1024]{1,0:T(8,128)S(1)}, f32[512,1024]{1,0:T(8,128)S(1)}) fusion(f32[1024]{0:T(1024)S(1)} %convert_add_fusion.5, f32[512]{0:T(512)S(1)} %bitcast.76), kind=kLoop, calls=%fused_computation.7.clone.1 | loop fusion | flops 524288 | bytes 4200448 | tf_op jit(solution)/shard_map/while/body/eval_jaxpr/cos | solution.py:24
  58.7 4.2 %fusion.52 = f32[512,64]{0,1:T(8,128)S(1)} fusion(f32[2048,64]{1,0:T(8,128)S(1)} %get-tuple-element.375, f32[512,1024]{1,0:T(8,128)S(1)} %get-tuple-element.334, f32[512,1024]{1,0:T(8,128)S(1)} %get-tuple-element.335), kind=kOutput, calls=%fused_computation.2.clone.1 | convolution fusion | flops 806354944 | bytes 4849664 | tf_op jit(solution)/shard_map/while/body/eval_jaxpr/dot_general | solution.py:32
  62.9 0.3 fusion.53
  63.3 7.3 %multiply_cosine_fusion.6 = (f32[512,1024]{1,0:T(8,128)S(1)}, f32[512,1024]{1,0:T(8,128)S(1)}) fusion(f32[1024]{0:T(1024)S(1)} %convert_add_fusion.5, f32[512]{0:T(512)S(1)} %bitcast.76), kind=kLoop, calls=%fused_computation.7.clone.1 | loop fusion | flops 524288 | bytes 4200448 | tf_op jit(solution)/shard_map/while/body/eval_jaxpr/cos | solution.py:24
  70.6 4.2 %fusion.52 = f32[512,64]{0,1:T(8,128)S(1)} fusion(f32[2048,64]{1,0:T(8,128)S(1)} %get-tuple-element.375, f32[512,1024]{1,0:T(8,128)S(1)} %get-tuple-element.334, f32[512,1024]{1,0:T(8,128)S(1)} %get-tuple-element.335), kind=kOutput, calls=%fused_computation.2.clone.1 | convolution fusion | flops 806354944 | bytes 4849664 | tf_op jit(solution)/shard_map/while/body/eval_jaxpr/dot_general | solution.py:32
  74.9 0.3 fusion.53
  75.3 7.3 %multiply_cosine_fusion.6 = (f32[512,1024]{1,0:T(8,128)S(1)}, f32[512,1024]{1,0:T(8,128)S(1)}) fusion(f32[1024]{0:T(1024)S(1)} %convert_add_fusion.5, f32[512]{0:T(512)S(1)} %bitcast.76), kind=kLoop, calls=%fused_computation.7.clone.1 | loop fusion | flops 524288 | bytes 4200448 | tf_op jit(solution)/shard_map/while/body/eval_jaxpr/cos | solution.py:24
  82.6 4.2 %fusion.52 = f32[512,64]{0,1:T(8,128)S(1)} fusion(f32[2048,64]{1,0:T(8,128)S(1)} %get-tuple-element.375, f32[512,1024]{1,0:T(8,128)S(1)} %get-tuple-element.334, f32[512,1024]{1,0:T(8,128)S(1)} %get-tuple-element.335), kind=kOutput, calls=%fused_computation.2.clone.1 | convolution fusion | flops 806354944 | bytes 4849664 | tf_op jit(solution)/shard_map/while/body/eval_jaxpr/dot_general | solution.py:32
  86.8 0.3 fusion.53
  87.2 7.3 %multiply_cosine_fusion.6 = (f32[512,1024]{1,0:T(8,128)S(1)}, f32[512,1024]{1,0:T(8,128)S(1)}) fusion(f32[1024]{0:T(1024)S(1)} %convert_add_fusion.5, f32[512]{0:T(512)S(1)} %bitcast.76), kind=kLoop, calls=%fused_computation.7.clone.1 | loop fusion | flops 524288 | bytes 4200448 | tf_op jit(solution)/shard_map/while/body/eval_jaxpr/cos | solution.py:24
  94.6 4.2 %fusion.52 = f32[512,64]{0,1:T(8,128)S(1)} fusion(f32[2048,64]{1,0:T(8,128)S(1)} %get-tuple-element.375, f32[512,1024]{1,0:T(8,128)S(1)} %get-tuple-element.334, f32[512,1024]{1,0:T(8,128)S(1)} %get-tuple-element.335), kind=kOutput, calls=%fused_computation.2.clone.1 | convolution fusion | flops 806354944 | bytes 4849664 | tf_op jit(solution)/shard_map/while/body/eval_jaxpr/dot_general | solution.py:32
  98.8 0.3 fusion.53
  99.2 119.2 %psum.7 = f32[2,2048]{1,0:T(2,128)S(1)} all-reduce(f32[2,2048]{1,0:T(2,128)S(1)} %bitcast.82), channel_id=1, replica_groups=mesh['pts'=16,'elem'=32] {'elem'}, use_global_device_ids=true, to_apply=%region_4.5 | all-reduce | flops 4096 | bytes 32768 | tf_op jit(solution)/shard_map/psum | solution.py:124
  218.3 0.0 copy-done.1
  218.4 0.0 copy-start
  218.4 0.0 copy-done.4
  218.4 0.5 copy-done
  219.0 42.9 %while.25 = (s32[]{:T(128)}, f32[1024,64]{0,1:T(8,128)S(1)}, f32[4,512]{1,0:T(4,128)S(1)}, f32[4,512]{1,0:T(4,128)S(1)}, f32[4,512]{1,0:T(4,128)S(1)}, /*index=5...) while((s32[]{:T(128)}, f32[1024,64]{0,1:T(8,128)S(1)}, f32[4,512]{1,0:T(4,128)S(1)}, ...), condition=%wide.region_6.7_spmd.clone, body=%wide.region_5.6_spmd.clone.sunk | while | flops 807291904 | bytes 10780911 | solution.py:98
  219.0 0.3 fusion.57
  219.3 7.3 %multiply_cosine_fusion.7 = (f32[512,1024]{1,0:T(8,128)S(1)}, f32[512,1024]{1,0:T(8,128)S(1)}) fusion(f32[1024]{0:T(1024)S(1)} %convert_add_fusion.6, f32[512]{0:T(512)S(1)} %bitcast.72), kind=kLoop, calls=%fused_computation.29.clone.1 | loop fusion | flops 524288 | bytes 4200448 | tf_op jit(solution)/shard_map/while/body/eval_jaxpr/cos | solution.py:54
  226.7 2.8 fusion.58
  229.6 0.1 maximum_add_fusion.2
  229.7 0.3 fusion.57
  230.1 7.3 %multiply_cosine_fusion.7 = (f32[512,1024]{1,0:T(8,128)S(1)}, f32[512,1024]{1,0:T(8,128)S(1)}) fusion(f32[1024]{0:T(1024)S(1)} %convert_add_fusion.6, f32[512]{0:T(512)S(1)} %bitcast.72), kind=kLoop, calls=%fused_computation.29.clone.1 | loop fusion | flops 524288 | bytes 4200448 | tf_op jit(solution)/shard_map/while/body/eval_jaxpr/cos | solution.py:54
  237.4 2.8 fusion.58
  240.3 0.1 maximum_add_fusion.2
  240.4 0.3 fusion.57
  240.8 7.3 %multiply_cosine_fusion.7 = (f32[512,1024]{1,0:T(8,128)S(1)}, f32[512,1024]{1,0:T(8,128)S(1)}) fusion(f32[1024]{0:T(1024)S(1)} %convert_add_fusion.6, f32[512]{0:T(512)S(1)} %bitcast.72), kind=kLoop, calls=%fused_computation.29.clone.1 | loop fusion | flops 524288 | bytes 4200448 | tf_op jit(solution)/shard_map/while/body/eval_jaxpr/cos | solution.py:54
  248.1 2.8 fusion.58
  251.0 0.1 maximum_add_fusion.2
  251.2 0.3 fusion.57
  251.5 7.3 %multiply_cosine_fusion.7 = (f32[512,1024]{1,0:T(8,128)S(1)}, f32[512,1024]{1,0:T(8,128)S(1)}) fusion(f32[1024]{0:T(1024)S(1)} %convert_add_fusion.6, f32[512]{0:T(512)S(1)} %bitcast.72), kind=kLoop, calls=%fused_computation.29.clone.1 | loop fusion | flops 524288 | bytes 4200448 | tf_op jit(solution)/shard_map/while/body/eval_jaxpr/cos | solution.py:54
  258.8 2.8 fusion.58
  261.7 0.1 maximum_add_fusion.2
  261.8 1.0 copy.26
  262.8 0.0 reduce-scatter.4.cloned.1.call-update
  262.9 66.2 %reduce-scatter.4.cloned.1.call-done = f32[64,64]{1,0:T(8,128)} async-done(((f32[1024,64]{1,0:T(8,128)}), f32[64,64]{1,0:T(8,128)}) %reduce-scatter.4.cloned.1.call-update) | async-done | bytes 16400 | tf_op jit(solution)/shard_map/reduce_scatter | solution.py:128
  329.1 0.9 fusion.34
  330.0 0.7 copy.25
  (40 shorter events, 0.5 us)
Async XLA Ops:
  7.2 321.9 %reduce-scatter.4.cloned.1.call-start = ((), (), s32[]{:S(2)}) async-start(), calls=%async_computation.1 | async-start | bytes 557056 | tf_op jit(solution)/shard_map/reduce_scatter | solution.py:128
  8.2 42.6 %copy-start.2 = (s32[2048]{0:T(1024)S(1)}, s32[2048]{0:T(1024)}, u32[]{:S(2)}) copy-start(s32[2048]{0:T(1024)} %param.13) | copy-start | bytes 24580
  8.3 42.6 %copy-start.3 = (s32[2048]{0:T(1024)S(1)}, s32[2048]{0:T(1024)}, u32[]{:S(2)}) copy-start(s32[2048]{0:T(1024)} %param.12) | copy-start | bytes 24580
  8.3 42.6 %copy-start.5 = (s32[32]{0:T(128)S(1)}, s32[32]{0:T(128)}, u32[]{:S(2)}) copy-start(s32[32]{0:T(128)} %param.11) | copy-start | bytes 388
  51.2 167.1 %copy-start.1 = (f32[2,2048]{1,0:T(2,128)S(1)}, f32[2,2048]{1,0:T(2,128)}, u32[]{:S(2)}) copy-start(f32[2,2048]{1,0:T(2,128)} %param.14) | copy-start | bytes 49156
  51.3 167.1 %copy-start.4 = (f32[2048]{0:T(1024)S(1)}, f32[2048]{0:T(1024)}, u32[]{:S(2)}) copy-start(f32[2048]{0:T(1024)} %param.15) | copy-start | bytes 24580
  218.4 0.6 copy-start
Sparse Core Ops, SparseCore 0:
  263.0 66.0 reduce-scatter.3
where the time goes:
time: 338 us
  blocking collectives  161 us (48%)
  waiting for transfers between devices  66.2 us (20%)
  other arithmetic  63.5 us (19%)
  matrix products  28.3 us (8%)
  between operations  14.2 us (4%)
  local copies, waits for them, and re-layouts  4.05 us (1%)
    psum x1, blocking collectives, shards(): total = lax.psum(partial_value, 'elem')  119 us
    reduce_scatter x1, waiting for transfers between devices, shards(): lax.psum_scatter(terms_blocks(slope_x, slope_y, q_re, q_im, lattice_x, co...  66.2 us
    all_gather x1, blocking collectives, shards(): whole = lax.all_gather(phasors, 'pts', axis=2, tiled=True)  41.7 us
    cos x4, other arithmetic, partial_field(): left = jnp.concatenate([jnp.cos(beam_y), jnp.sin(beam_y)], 1)  29.4 us
    cos x4, other arithmetic, surface_terms(): left = jnp.concatenate([jnp.cos(beam_y), jnp.sin(beam_y)], 1)  29.4 us
    dot_general x4, matrix products, partial_field(): jnp.dot(left, right, precision=HIGH, preferred_element_type=jnp.float32)  16.9 us
    dot_general x4, matrix products, surface_terms(): lax.dot_general(left, right, (((0,), (0,)), ((), ())), precision=HIGH, pr...  11.4 us
  transfers between devices with their start and end apart: 1, of which 1 were waited for; matrix products, arithmetic and copies ran while one was open for 0% of the time, Pallas kernels for 0%

commit v1 on v0

v1 whole, which is shorter than its diff:
```python
import math

import jax
import jax.numpy as jnp
from jax import lax
from jax.experimental import pallas as pl
from jax.experimental.pallas import tpu as pltpu
from jax.sharding import PartitionSpec as P

NX_EL = 1024
NY_EL = 1024
CHUNKS = 4
CW = 512
LOW = 128
TWO_PI = 2.0 * math.pi

F32 = jnp.float32
BF16 = jnp.bfloat16


def _fit(func, degree):
    import numpy as np

    nodes = 0.125 + 0.125 * np.cos(np.pi * (np.arange(64) + 0.5) / 64)
    poly = np.polynomial.Chebyshev.fit(nodes, func(np.sqrt(nodes)), degree, domain=[0.0, 0.25])
    return [float(c) for c in poly.convert(kind=np.polynomial.Polynomial).coef]


def _tables():
    import numpy as np

    return (
        _fit(lambda r: np.sin(np.pi * r) / r, 5),
        _fit(lambda r: np.cos(np.pi * r), 5),
    )


SIN_C, COS_C = _tables()


def _horner(x, coefs):
    acc = jnp.full_like(x, coefs[-1])
    for c in coefs[-2::-1]:
        acc = acc * x + c
    return acc


def cos_sin_turns(t):
    r = t - jnp.round(t)
    x = r * r
    s = r * _horner(x, SIN_C)
    c = _horner(x, COS_C)
    two_s = s + s
    return 1.0 - two_s * s, two_s * c


def split(x):
    hi = x.astype(BF16)
    lo = (x - hi.astype(F32)).astype(BF16)
    return hi, lo


def mm(a, b):
    return lax.dot_general(a, b, (((1,), (0,)), ((), ())), preferred_element_type=F32)


def mm_nt(a, b):
    return lax.dot_general(a, b, (((1,), (1,)), ((), ())), preferred_element_type=F32)


def slopes(rows_ref, cols_ref):
    along_x = (rows_ref[...].astype(F32) - 255.5) * 0.5
    along_y = (cols_ref[...].astype(F32) - 127.5) * 0.5
    radius = jnp.sqrt(along_x * along_x + along_y * along_y + 1600.0)
    return along_x / radius, along_y / radius, 80.0 / (radius * 1024.0)


def sides(v):
    out = []
    for h in range(NY_EL // LOW):
        a = v[2 * h]
        b = v[2 * h + 1]
        top = jnp.concatenate([a[:, :64], b[:, :64]], 1)
        low = jnp.concatenate([a[:, 64:], b[:, 64:]], 1)
        out.append(jnp.concatenate([top, low], 0))
    return out


def table_kernel(prow_ref, pcol_ref, rows_ref, low_ref, high_ref, x_ref):
    sx, sy, _ = slopes(prow_ref, pcol_ref)
    sx = sx * 0.5
    sy = sy * 0.5
    low_k = lax.broadcasted_iota(jnp.int32, (LOW, CW), 0).astype(F32) - (LOW - 1) / 2.0
    high_k = (lax.broadcasted_iota(jnp.int32, (8, CW), 0) * LOW).astype(F32) + LOW / 2.0
    lattice_x = rows_ref[...].astype(F32) - (NX_EL - 1) / 2.0
    for r in range(CHUNKS):
        cols = slice(CW * r, CW * r + CW)
        c, s = cos_sin_turns(low_k * sy[r : r + 1])
        hi, lo = split(c)
        low_ref[0:LOW, cols] = hi
        low_ref[2 * LOW : 3 * LOW, cols] = lo
        hi, lo = split(s)
        low_ref[LOW : 2 * LOW, cols] = hi
        low_ref[3 * LOW : 4 * LOW, cols] = lo
        c, s = cos_sin_turns(high_k * sy[r : r + 1])
        high_ref[0:4, cols] = c[0:4]
        high_ref[4:8, cols] = s[0:4]
        c, s = cos_sin_turns(lattice_x * sx[r : r + 1])
        x_ref[0:32, cols] = c
        x_ref[32:64, cols] = s


def field_kernel(theta_ref, low_ref, high_ref, x_ref, part_ref, u_ref):
    c, s = cos_sin_turns(theta_ref[...] * (1.0 / TWO_PI))
    re = sides(c)
    im = sides(s)
    rows = []
    for g in range(4):
        for sign in (1.0, -1.0):
            v_re = re[4 + g] + sign * re[3 - g]
            v_im = im[4 + g] + sign * im[3 - g]
            rows.append(jnp.concatenate([v_re, -v_im], 1))
            rows.append(jnp.concatenate([v_im, v_re], 1))
    for h in range(8):
        u_ref[0:32, 128 * h : 128 * h + 128] = re[h]
        u_ref[32:64, 128 * h : 128 * h + 128] = im[h]
    hi, lo = split(jnp.concatenate(rows, 0))
    both = jnp.concatenate([hi, hi], 1)
    for r in range(CHUNKS):
        cols = slice(CW * r, CW * r + CW)
        p = mm(both, low_ref[:, cols]) + mm(lo, low_ref[0 : 2 * LOW, cols])
        f_re = jnp.zeros((32, CW), F32)
        f_im = jnp.zeros((32, CW), F32)
        for g in range(4):
            hc = high_ref[g : g + 1, cols]
            hs = high_ref[4 + g : 5 + g, cols]
            q = p[128 * g : 128 * g + 128]
            f_re = f_re + (hc * q[0:32] - hs * q[96:128])
            f_im = f_im + (hc * q[32:64] + hs * q[64:96])
        xc = x_ref[0:32, cols]
        xs = x_ref[32:64, cols]
        part_ref[r : r + 1] = jnp.sum(xc * f_re - xs * f_im, 0, keepdims=True)
        part_ref[r + 4 : r + 5] = jnp.sum(xc * f_im + xs * f_re, 0, keepdims=True)


def gradient_kernel(
    parts_ref, direct_ref, noise_ref, prow_ref, pcol_ref, low_ref, high_ref, x_ref, u_ref, field_ref, out_ref, whi_ref, wlo_ref
):
    _, _, scale = slopes(prow_ref, pcol_ref)
    total = jnp.sum(parts_ref[...], 0)
    re = direct_ref[0:4] + scale * total[0:4]
    im = direct_ref[4:8] + scale * total[4:8]
    field_ref[0:4] = re
    field_ref[4:8] = im
    power = noise_ref[...] + re * re + im * im
    q_re = re * scale / power
    q_im = -im * scale / power
    for r in range(CHUNKS):
        cols = slice(CW * r, CW * r + CW)
        a = q_re[r : r + 1]
        b = q_im[r : r + 1]
        xc = x_ref[0:32, cols]
        xs = x_ref[32:64, cols]
        w_re = a * xc - b * xs
        w_im = a * xs + b * xc
        w = jnp.concatenate([w_re, w_im], 0)
        for g in range(4):
            hi, lo = split(w * high_ref[g : g + 1, cols])
            whi_ref[128 * g : 128 * g + 64, cols] = hi
            wlo_ref[128 * g : 128 * g + 64, cols] = lo
            hi, lo = split(w * high_ref[4 + g : 5 + g, cols])
            whi_ref[128 * g + 64 : 128 * g + 128, cols] = hi
            wlo_ref[128 * g + 64 : 128 * g + 128, cols] = lo
    sums = (
        mm_nt(whi_ref[...], low_ref[0 : 2 * LOW])
        + mm_nt(wlo_ref[...], low_ref[0 : 2 * LOW])
        + mm_nt(whi_ref[...], low_ref[2 * LOW :])
    )
    for g in range(4):
        v = sums[128 * g : 128 * g + 128]
        a_re = v[0:32, :LOW] - v[32:64, LOW:]
        a_im = v[0:32, LOW:] + v[32:64, :LOW]
        b_re = v[64:96, :LOW] - v[96:128, LOW:]
        b_im = v[64:96, LOW:] + v[96:128, :LOW]
        for h, s_re, s_im in ((4 + g, a_re - b_im, a_im + b_re), (3 - g, a_re + b_im, a_im - b_re)):
            cols = slice(128 * h, 128 * h + 128)
            d = -2.0 * (u_ref[0:32, cols] * s_im + u_ref[32:64, cols] * s_re)
            out_ref[2 * h] = jnp.concatenate([d[:16, :64], d[16:, :64]], 1)
            out_ref[2 * h + 1] = jnp.concatenate([d[:16, 64:], d[16:, 64:]], 1)


def pack(block):
    return jnp.concatenate([block[:16], block[16:]], 1)


def shards(theta, panel_rows, point_rows, point_cols, direct, noise):
    points = point_rows.shape[0]
    peers = lax.axis_size("pts")
    elems = lax.axis_size("elem")
    params = pltpu.CompilerParams(vmem_limit_bytes=40 << 20)
    sent = jnp.broadcast_to(pack(theta)[None], (peers, 16, 128))
    angles = lax.all_to_all(sent, "pts", 0, 0, tiled=True)
    prow = point_rows.reshape(CHUNKS, CW)
    pcol = point_cols.reshape(CHUNKS, CW)
    direct = direct.reshape(8, CW)
    noise = noise.reshape(CHUNKS, CW)
    low, high, beam = pl.pallas_call(
        table_kernel,
        out_shape=(
            jax.ShapeDtypeStruct((4 * LOW, points), BF16),
            jax.ShapeDtypeStruct((8, points), F32),
            jax.ShapeDtypeStruct((64, points), F32),
        ),
        compiler_params=params,
        name="tables",
    )(prow, pcol, panel_rows.reshape(32, 1))
    part, phasors = pl.pallas_call(
        field_kernel,
        out_shape=(
            jax.ShapeDtypeStruct((8, CW), F32),
            jax.ShapeDtypeStruct((64, NY_EL), F32),
        ),
        compiler_params=params,
        name="field",
    )(angles, low, high, beam)
    part, direct, noise = lax.optimization_barrier((part, direct, noise))
    parts = lax.all_to_all(jnp.broadcast_to(part[None], (elems, 8, CW)), "elem", 0, 0, tiled=True)
    field, grads = pl.pallas_call(
        gradient_kernel,
        out_shape=(
            jax.ShapeDtypeStruct((8, CW), F32),
            jax.ShapeDtypeStruct((peers, 16, 128), F32),
        ),
        scratch_shapes=[pltpu.VMEM((512, points), BF16), pltpu.VMEM((512, points), BF16)],
        compiler_params=params,
        name="gradient",
    )(parts, direct, noise, prow, pcol, low, high, beam, phasors)
    field, grads = lax.optimization_barrier((field.reshape(2, points), grads))
    total = jnp.sum(lax.all_to_all(grads, "pts", 0, 0, tiled=True), 0)
    grad = jnp.concatenate([total[:, :64], total[:, 64:]], 0)
    return grad, field


def solution(mesh):
    in_specs = (P("elem", "pts"), P("elem"), P("pts"), P("pts"), P(None, "pts"), P("pts"))
    out_specs = (P("elem", "pts"), P(None, "pts"))
    return jax.shard_map(shards, mesh=mesh, in_specs=in_specs, out_specs=out_specs, check_vma=False)
```

time: 338 us -> 74.3 us (0.22)
  the two profiles are of different devices: /device:TPU:2 before, /device:TPU:32 now
where the time goes in v1:
time: 74.3 us; the launch traced here: 73.6 us
  blocking collectives  36.7 us (49%)
  starting transfers between devices  15.2 us (20%)
  waiting for transfers between devices  8.36 us (11%)
  Pallas kernels  6.21 us (8%)
  local copies, waits for them, and re-layouts  5.71 us (8%)
    all_to_all x1, blocking collectives, shards(): lax.all_to_all(jnp.broadcast_to(part[None], (elems, 8, CW)), 'elem', 0, 0...  18.7 us
    all_to_all x1, blocking collectives, shards(): total = jnp.sum(lax.all_to_all(grads, 'pts', 0, 0, tiled=True), 0)  18 us
    all_to_all x1, starting transfers between devices, shards(): angles = lax.all_to_all(sent, 'pts', 0, 0, tiled=True)  15.2 us
    all_to_all x1, waiting for transfers between devices, shards(): angles = lax.all_to_all(sent, 'pts', 0, 0, tiled=True)  8.36 us
    pallas_call x1, Pallas kernels, shards(): pl.pallas_call(table_kernel, out_shape=(jax.ShapeDtypeStruct((4 * LOW, po...  2.27 us
    pallas_call x1, Pallas kernels, shards(): pl.pallas_call(gradient_kernel, out_shape=(jax.ShapeDtypeStruct((8, CW),...  1.98 us
    pallas_call x1, Pallas kernels, shards(): pl.pallas_call(field_kernel, out_shape=(jax.ShapeDtypeStruct((8, CW), F32...  1.95 us
  transfers between devices with their start and end apart: 1, of which 1 were waited for; matrix products, arithmetic and copies ran while one was open for 5% of the time, Pallas kernels for 3%

profile of v1, /device:TPU:32, one launch (start us, length us, event | category | flops | bytes accessed | tf_op | source)
XLA Modules:
  0.0 73.6 jit_solution(17398225741952263154)
XLA Ops:
  0.6 0.7 fusion
  1.3 0.1 pad_maximum_fusion.1
  1.4 0.7 broadcast_in_dim.4
  2.1 15.2 %all-to-all-start = ((f32[16,16,128]{2,1,0:T(8,128)}), f32[16,16,128]{2,1,0:T(8,128)S(1)}, u32[]{:S(2)}, u32[]{:S(2)}) async-start(f32[16,16,128]{2,1,0:T(8,128)} %broadcast_in_dim.4), calls=%async_computation | async-start | bytes 262144 | tf_op jit(solution)/shard_map/all_to_all | solution.py:202
  17.3 0.7 reshape.24.prow_ref
  18.0 0.7 reshape.25.pcol_ref
  18.7 0.7 reshape.28.noise_ref
  19.4 0.7 copy.8.rows_ref
  20.1 0.7 reshape.27.direct_ref
  20.9 2.3 %tables.1 = (bf16[512,2048]{1,0:T(8,128)(2,1)S(1)}, f32[8,2048]{1,0:T(8,128)S(1)}, f32[64,2048]{1,0:T(8,128)S(1)}) custom-call(s32[4,512]{1,0:T(4,128)S(1)} %reshape.24.prow_ref, s32[4,512]{1,0:T(4,128)S(1)} %reshape.25.pcol_ref, s32[32,1]{1,0:T(8,128)S(1)} %copy.8.rows_ref), custom_call_target="tpu_custom_call" | custom-call | tf_op jit(solution)/shard_map/tables/pallas_call | solution.py:207
  23.2 8.4 %all-to-all-done.theta_ref = f32[16,16,128]{2,1,0:T(8,128)S(1)} async-done(((f32[16,16,128]{2,1,0:T(8,128)}), f32[16,16,128]{2,1,0:T(8,128)S(1)}, u32[]{:S(2)}, u32[]{:S(2)}) %all-to-all-start) | async-done | bytes 131104 | tf_op jit(solution)/shard_map/all_to_all | solution.py:202
  31.5 1.9 %field.1 = (f32[8,512]{1,0:T(8,128)S(1)}, f32[64,1024]{1,0:T(8,128)S(1)}) custom-call(f32[16,16,128]{2,1,0:T(8,128)S(1)} %all-to-all-done.theta_ref, bf16[512,2048]{1,0:T(8,128)(2,1)S(1)} %get-tuple-element.14.low_ref, f32[8,2048]{1,0:T(8,128)S(1)} %get-tuple-element.15.high_ref, f32[64,2048]{1,0:T(8,128)S(1)} %get-tuple-element.16.x_ref), custom_call_target="tpu_custom_call" | custom-call | tf_op jit(solution)/shard_map/field/pallas_call | solution.py:217
  33.5 0.1 broadcast_in_dim.5
  33.5 18.7 %all_to_all.15.parts_ref = f32[32,8,512]{2,1,0:T(8,128)S(1)} all-to-all(f32[32,8,512]{2,1,0:T(8,128)S(1)} %broadcast_in_dim.5), channel_id=1, replica_groups=mesh['pts'=16,'elem'=32] {'elem'}, dimensions={0} | all-to-all | bytes 1048576 | tf_op jit(solution)/shard_map/all_to_all | solution.py:227
  52.2 2.0 %gradient.1 = (f32[8,512]{1,0:T(8,128)S(1)}, f32[16,16,128]{2,1,0:T(8,128)S(1)}) custom-call(f32[32,8,512]{2,1,0:T(8,128)S(1)} %all_to_all.15.parts_ref, f32[8,512]{1,0:T(8,128)S(1)} %reshape.27.direct_ref, f32[4,512]{1,0:T(4,128)S(1)} %reshape.28.noise_ref, s32[4,512]{1,0:T(4,128)S(1)} %reshape.24.prow_ref, s32[4,512]{1,0:T(4,128)S(1)} %reshape.25.pcol_ref, ...), custom_call_target="tpu_custom_call" | custom-call | tf_op jit(solution)/shard_map/gradient/pallas_call | solution.py:228
  54.2 0.6 reshape.29
  54.9 18.0 %all_to_all.16 = f32[16,16,128]{2,1,0:T(8,128)S(1)} all-to-all(f32[16,16,128]{2,1,0:T(8,128)S(1)} %get-tuple-element.24), channel_id=1, replica_groups=mesh['pts'=16,'elem'=32] {'pts'}, dimensions={0} | all-to-all | bytes 262144 | tf_op jit(solution)/shard_map/all_to_all | solution.py:239
  72.9 0.1 fusion.1
  73.0 0.6 pad_maximum_fusion
  (1 shorter events, 0.0 us)
Async XLA Ops:
  2.1 29.4 %all-to-all-start = ((f32[16,16,128]{2,1,0:T(8,128)}), f32[16,16,128]{2,1,0:T(8,128)S(1)}, u32[]{:S(2)}, u32[]{:S(2)}) async-start(f32[16,16,128]{2,1,0:T(8,128)} %broadcast_in_dim.4), calls=%async_computation | async-start | bytes 262144 | tf_op jit(solution)/shard_map/all_to_all | solution.py:202

commit v2 on v1

--- a/solution.py
+++ b/solution.py
@@ -11,6 +11,8 @@
 NY_EL = 1024
 CHUNKS = 4
 CW = 512
+TURN_IN = 10
+TURN_OUT = 10
 LOW = 128
 TWO_PI = 2.0 * math.pi
 
@@ -68,6 +70,15 @@
     return lax.dot_general(a, b, (((1,), (1,)), ((), ())), preferred_element_type=F32)
 
 
+def flip(x):
+    i = lax.broadcasted_iota(jnp.int32, (LOW, LOW), 0)
+    j = lax.broadcasted_iota(jnp.int32, (LOW, LOW), 1)
+    anti = jnp.where(i + j == LOW - 1, 1.0, 0.0).astype(BF16)
+    hi, lo = split(x)
+    r = mm(jnp.concatenate([hi, lo], 0), anti)
+    return r[: x.shape[0]] + r[x.shape[0] :]
+
+
 def slopes(rows_ref, cols_ref):
     along_x = (rows_ref[...].astype(F32) - 255.5) * 0.5
     along_y = (cols_ref[...].astype(F32) - 127.5) * 0.5
@@ -78,20 +89,27 @@
 def sides(v):
     out = []
     for h in range(NY_EL // LOW):
-        a = v[2 * h]
-        b = v[2 * h + 1]
+        a = v[(2 * h - TURN_IN) % 16]
+        b = v[(2 * h + 1 - TURN_IN) % 16]
         top = jnp.concatenate([a[:, :64], b[:, :64]], 1)
         low = jnp.concatenate([a[:, 64:], b[:, 64:]], 1)
         out.append(jnp.concatenate([top, low], 0))
     return out
 
 
+def pack_kernel(theta_ref, out_ref):
+    v = theta_ref[...]
+    v = jnp.concatenate([v[:16], v[16:]], 1)
+    for z in range(out_ref.shape[0]):
+        out_ref[z] = v
+
+
 def table_kernel(prow_ref, pcol_ref, rows_ref, low_ref, high_ref, x_ref):
     sx, sy, _ = slopes(prow_ref, pcol_ref)
     sx = sx * 0.5
     sy = sy * 0.5
-    low_k = lax.broadcasted_iota(jnp.int32, (LOW, CW), 0).astype(F32) - (LOW - 1) / 2.0
-    high_k = (lax.broadcasted_iota(jnp.int32, (8, CW), 0) * LOW).astype(F32) + LOW / 2.0
+    low_k = lax.broadcasted_iota(jnp.int32, (LOW, CW), 0).astype(F32) + 0.5
+    high_k = (lax.broadcasted_iota(jnp.int32, (8, CW), 0) * (2 * LOW)).astype(F32) + LOW
     lattice_x = rows_ref[...].astype(F32) - (NX_EL - 1) / 2.0
     for r in range(CHUNKS):
         cols = slice(CW * r, CW * r + CW)
@@ -114,24 +132,37 @@
     c, s = cos_sin_turns(theta_ref[...] * (1.0 / TWO_PI))
     re = sides(c)
     im = sides(s)
+    back = flip(jnp.concatenate([re[0], im[0], re[2], im[2], re[4], im[4], re[6], im[6]], 0))
+    even_re, even_im, odd_re, odd_im = [], [], [], []
+    for h in range(4):
+        m_re = back[64 * h : 64 * h + 32]
+        m_im = back[64 * h + 32 : 64 * h + 64]
+        p_re = re[2 * h + 1]
+        p_im = im[2 * h + 1]
+        cols = slice(LOW * 2 * h, LOW * 2 * h + LOW)
+        u_ref[0:32, cols] = m_re
+        u_ref[32:64, cols] = m_im
+        cols = slice(LOW * (2 * h + 1), LOW * (2 * h + 2))
+        u_ref[0:32, cols] = p_re
+        u_ref[32:64, cols] = p_im
+        even_re.append(p_re + m_re)
+        even_im.append(p_im + m_im)
+        odd_re.append(p_re - m_re)
+        odd_im.append(p_im - m_im)
     rows = []
-    for g in range(4):
+    for g in range(2):
         for sign in (1.0, -1.0):
-            v_re = re[4 + g] + sign * re[3 - g]
-            v_im = im[4 + g] + sign * im[3 - g]
-            rows.append(jnp.concatenate([v_re, -v_im], 1))
-            rows.append(jnp.concatenate([v_im, v_re], 1))
-    for h in range(8):
-        u_ref[0:32, 128 * h : 128 * h + 128] = re[h]
-        u_ref[32:64, 128 * h : 128 * h + 128] = im[h]
+            e_re, e_im, o_re, o_im = (v[2 + g] + sign * v[1 - g] for v in (even_re, even_im, odd_re, odd_im))
+            rows.append(jnp.concatenate([e_re, -o_im], 1))
+            rows.append(jnp.concatenate([e_im, o_re], 1))
     hi, lo = split(jnp.concatenate(rows, 0))
-    both = jnp.concatenate([hi, hi], 1)
+    left = jnp.concatenate([hi, hi, lo], 1)
     for r in range(CHUNKS):
         cols = slice(CW * r, CW * r + CW)
-        p = mm(both, low_ref[:, cols]) + mm(lo, low_ref[0 : 2 * LOW, cols])
+        p = mm(left, jnp.concatenate([low_ref[:, cols], low_ref[0 : 2 * LOW, cols]], 0))
         f_re = jnp.zeros((32, CW), F32)
         f_im = jnp.zeros((32, CW), F32)
-        for g in range(4):
+        for g in range(2):
             hc = high_ref[g : g + 1, cols]
             hs = high_ref[4 + g : 5 + g, cols]
             q = p[128 * g : 128 * g + 128]
@@ -144,14 +175,18 @@
 
 
 def gradient_kernel(
-    parts_ref, direct_ref, noise_ref, prow_ref, pcol_ref, low_ref, high_ref, x_ref, u_ref, field_ref, out_ref, whi_ref, wlo_ref
+    parts_ref, direct_ref, noise_ref, prow_ref, pcol_ref, low_ref, high_ref, x_ref, u_ref, field_ref, out_ref, held_ref, whi_ref, wlo_ref, sem
 ):
     _, _, scale = slopes(prow_ref, pcol_ref)
     total = jnp.sum(parts_ref[...], 0)
     re = direct_ref[0:4] + scale * total[0:4]
     im = direct_ref[4:8] + scale * total[4:8]
-    field_ref[0:4] = re
-    field_ref[4:8] = im
+    for r in range(CHUNKS):
+        cols = slice(CW * r, CW * r + CW)
+        held_ref[0:1, cols] = re[r : r + 1]
+        held_ref[1:2, cols] = im[r : r + 1]
+    copy = pltpu.make_async_copy(held_ref, field_ref, sem)
+    copy.start()
     power = noise_ref[...] + re * re + im * im
     q_re = re * scale / power
     q_im = -im * scale / power
@@ -164,7 +199,7 @@
         w_re = a * xc - b * xs
         w_im = a * xs + b * xc
         w = jnp.concatenate([w_re, w_im], 0)
-        for g in range(4):
+        for g in range(2):
             hi, lo = split(w * high_ref[g : g + 1, cols])
             whi_ref[128 * g : 128 * g + 64, cols] = hi
             wlo_ref[128 * g : 128 * g + 64, cols] = lo
@@ -176,21 +211,33 @@
         + mm_nt(wlo_ref[...], low_ref[0 : 2 * LOW])
         + mm_nt(whi_ref[...], low_ref[2 * LOW :])
     )
-    for g in range(4):
+    blocks = [None] * 8
+    for g in range(2):
         v = sums[128 * g : 128 * g + 128]
-        a_re = v[0:32, :LOW] - v[32:64, LOW:]
-        a_im = v[0:32, LOW:] + v[32:64, :LOW]
-        b_re = v[64:96, :LOW] - v[96:128, LOW:]
-        b_im = v[64:96, LOW:] + v[96:128, :LOW]
-        for h, s_re, s_im in ((4 + g, a_re - b_im, a_im + b_re), (3 - g, a_re + b_im, a_im - b_re)):
-            cols = slice(128 * h, 128 * h + 128)
-            d = -2.0 * (u_ref[0:32, cols] * s_im + u_ref[32:64, cols] * s_re)
-            out_ref[2 * h] = jnp.concatenate([d[:16, :64], d[16:, :64]], 1)
-            out_ref[2 * h + 1] = jnp.concatenate([d[:16, 64:], d[16:, 64:]], 1)
-
-
-def pack(block):
-    return jnp.concatenate([block[:16], block[16:]], 1)
+        cc = v[0:64, :LOW]
+        cs = v[0:64, LOW:]
+        sc = v[64:128, :LOW]
+        ss = v[64:128, LOW:]
+        minus = cc - ss
+        plus = cc + ss
+        added = cs + sc
+        taken = cs - sc
+        for n, real, imag in (
+            (5 + 2 * g, minus, added),
+            (4 + 2 * g, plus, -taken),
+            (3 - 2 * g, plus, taken),
+            (2 - 2 * g, minus, -added),
+        ):
+            s_re = real[:32] - imag[32:]
+            s_im = real[32:] + imag[:32]
+            cols = slice(LOW * n, LOW * n + LOW)
+            blocks[n] = -2.0 * (u_ref[0:32, cols] * s_im + u_ref[32:64, cols] * s_re)
+    back = flip(jnp.concatenate(blocks[0::2], 0))
+    for n in range(8):
+        d = blocks[n] if n % 2 else back[16 * n : 16 * n + 32]
+        out_ref[(2 * n - TURN_OUT) % 16] = jnp.concatenate([d[:16, :64], d[16:, :64]], 1)
+        out_ref[(2 * n + 1 - TURN_OUT) % 16] = jnp.concatenate([d[:16, 64:], d[16:, 64:]], 1)
+    copy.wait()
 
 
 def shards(theta, panel_rows, point_rows, point_cols, direct, noise):
@@ -198,8 +245,16 @@
     peers = lax.axis_size("pts")
     elems = lax.axis_size("elem")
     params = pltpu.CompilerParams(vmem_limit_bytes=40 << 20)
-    sent = jnp.broadcast_to(pack(theta)[None], (peers, 16, 128))
-    angles = lax.all_to_all(sent, "pts", 0, 0, tiled=True)
+    sent = pl.pallas_call(
+        pack_kernel,
+        out_shape=jax.ShapeDtypeStruct((peers, 16, 128), F32),
+        compiler_params=params,
+        name="pack",
+    )(theta)
+    along_in = [[(i + TURN_IN) % peers for i in range(peers)]]
+    along_out = [[(i + TURN_OUT) % peers for i in range(peers)]]
+    plane = [[(i + 21) % elems for i in range(elems)]]
+    angles = lax.all_to_all(sent, "pts", 0, 0, axis_index_groups=along_in, tiled=True)
     prow = point_rows.reshape(CHUNKS, CW)
     pcol = point_cols.reshape(CHUNKS, CW)
     direct = direct.reshape(8, CW)
@@ -224,19 +279,24 @@
         name="field",
     )(angles, low, high, beam)
     part, direct, noise = lax.optimization_barrier((part, direct, noise))
-    parts = lax.all_to_all(jnp.broadcast_to(part[None], (elems, 8, CW)), "elem", 0, 0, tiled=True)
+    parts = lax.all_to_all(jnp.broadcast_to(part[None], (elems, 8, CW)), "elem", 0, 0, axis_index_groups=plane, tiled=True)
     field, grads = pl.pallas_call(
         gradient_kernel,
         out_shape=(
-            jax.ShapeDtypeStruct((8, CW), F32),
+            jax.ShapeDtypeStruct((2, points), F32),
             jax.ShapeDtypeStruct((peers, 16, 128), F32),
         ),
-        scratch_shapes=[pltpu.VMEM((512, points), BF16), pltpu.VMEM((512, points), BF16)],
+        out_specs=(pl.BlockSpec(memory_space=pl.ANY), pl.BlockSpec(memory_space=pltpu.VMEM)),
+        scratch_shapes=[
+            pltpu.VMEM((2, points), F32),
+            pltpu.VMEM((256, points), BF16),
+            pltpu.VMEM((256, points), BF16),
+            pltpu.SemaphoreType.DMA,
+        ],
         compiler_params=params,
         name="gradient",
     )(parts, direct, noise, prow, pcol, low, high, beam, phasors)
-    field, grads = lax.optimization_barrier((field.reshape(2, points), grads))
-    total = jnp.sum(lax.all_to_all(grads, "pts", 0, 0, tiled=True), 0)
+    total = jnp.sum(lax.all_to_all(grads, "pts", 0, 0, axis_index_groups=along_out, tiled=True), 0)
     grad = jnp.concatenate([total[:, :64], total[:, 64:]], 0)
     return grad, field
 

time: 74.3 us -> 65.9 us (0.89)
  the two profiles are of different devices: /device:TPU:32 before, /device:TPU:2 now
where the time goes in v2:
time: 65.9 us; the launch traced here: 65.3 us
  blocking collectives  34.1 us (52%)
  starting transfers between devices  17.1 us (26%)
  Pallas kernels  6.1 us (9%)
  local copies, waits for them, and re-layouts  4.42 us (7%)
  waiting for transfers between devices  2.35 us (4%)
  between operations  0.68 us (1%)
    all_to_all x1, blocking collectives, shards(): lax.all_to_all(grads, 'pts', 0, 0, axis_index_groups=along_out, tiled=True)  19 us
    all_to_all x1, starting transfers between devices, shards(): lax.all_to_all(sent, 'pts', 0, 0, axis_index_groups=along_in, tiled=True)  17.1 us
    all_to_all x1, blocking collectives, shards(): lax.all_to_all(jnp.broadcast_to(part[None], (elems, 8, CW)), 'elem', 0, 0...  15.1 us
    all_to_all x1, waiting for transfers between devices, shards(): lax.all_to_all(sent, 'pts', 0, 0, axis_index_groups=along_in, tiled=True)  2.35 us
    pallas_call x1, Pallas kernels, shards(): pl.pallas_call(table_kernel, out_shape=(jax.ShapeDtypeStruct((4 * LOW, po...  2.27 us
    pallas_call x1, Pallas kernels, shards(): pl.pallas_call(gradient_kernel, out_shape=(jax.ShapeDtypeStruct((2, point...  1.83 us
  transfers between devices with their start and end apart: 1, of which 1 were waited for; matrix products, arithmetic and copies ran while one was open for 5% of the time, Pallas kernels for 3%

profile of v2, /device:TPU:2, one launch (start us, length us, event | category | flops | bytes accessed | tf_op | source)
XLA Modules:
  0.0 65.3 jit_solution(2782468965503603919)
XLA Ops:
  0.6 0.0 copy-start
  0.6 0.7 %copy-done = f32[32,64]{1,0:T(8,128)S(1)} copy-done((f32[32,64]{1,0:T(8,128)S(1)}, f32[32,64]{1,0:T(8,128)}, u32[]{:S(2)}) %copy-start) | copy-done | bytes 8216
  1.3 0.7 %pack.1 = f32[16,16,128]{2,1,0:T(8,128)} custom-call(f32[32,64]{1,0:T(8,128)S(1)} %copy-done), custom_call_target="tpu_custom_call" | custom-call | tf_op jit(solution)/shard_map/pack/pallas_call | solution.py:248
  2.1 17.1 %all-to-all-start = ((f32[16,16,128]{2,1,0:T(8,128)}), f32[16,16,128]{2,1,0:T(8,128)S(1)}, u32[]{:S(2)}, u32[]{:S(2)}) async-start(f32[16,16,128]{2,1,0:T(8,128)} %pack.1), calls=%async_computation | async-start | bytes 262144 | tf_op jit(solution)/shard_map/all_to_all | solution.py:257
  19.1 0.7 %reshape.20.prow_ref = s32[4,512]{1,0:T(4,128)S(1)} reshape(s32[2048]{0:T(1024)} %param.8) | data formatting | bytes 16384 | tf_op jit(solution)/shard_map/reshape | solution.py:258
  19.8 0.7 %reshape.21.pcol_ref = s32[4,512]{1,0:T(4,128)S(1)} reshape(s32[2048]{0:T(1024)} %param.9) | data formatting | bytes 16384 | tf_op jit(solution)/shard_map/reshape | solution.py:259
  20.5 0.7 %reshape.24.noise_ref = f32[4,512]{1,0:T(4,128)S(1)} reshape(f32[2048]{0:T(1024)} %param.11) | data formatting | bytes 16384 | tf_op jit(solution)/shard_map/reshape | solution.py:261
  21.2 0.7 %copy.8.rows_ref = s32[32,1]{1,0:T(8,128)S(1)} copy(s32[32,1]{0,1:T(1,128)} %bitcast.1) | data formatting | bytes 256 | tf_op jit(solution)/shard_map/reshape | solution.py:271
  22.0 0.7 %reshape.23.direct_ref = f32[8,512]{1,0:T(8,128)S(1)} reshape(f32[2,2048]{1,0:T(2,128)} %param.10) | data formatting | bytes 32768 | tf_op jit(solution)/shard_map/reshape | solution.py:260
  22.7 2.3 %tables.1 = (bf16[512,2048]{1,0:T(8,128)(2,1)S(1)}, f32[8,2048]{1,0:T(8,128)S(1)}, f32[64,2048]{1,0:T(8,128)S(1)}) custom-call(s32[4,512]{1,0:T(4,128)S(1)} %reshape.20.prow_ref, s32[4,512]{1,0:T(4,128)S(1)} %reshape.21.pcol_ref, s32[32,1]{1,0:T(8,128)S(1)} %copy.8.rows_ref), custom_call_target="tpu_custom_call" | custom-call | tf_op jit(solution)/shard_map/tables/pallas_call | solution.py:262
  25.0 2.4 %all-to-all-done.theta_ref = f32[16,16,128]{2,1,0:T(8,128)S(1)} async-done(((f32[16,16,128]{2,1,0:T(8,128)}), f32[16,16,128]{2,1,0:T(8,128)S(1)}, u32[]{:S(2)}, u32[]{:S(2)}) %all-to-all-start) | async-done | bytes 131104 | tf_op jit(solution)/shard_map/all_to_all | solution.py:257
  27.3 1.3 %field.1 = (f32[8,512]{1,0:T(8,128)S(1)}, f32[64,1024]{1,0:T(8,128)S(1)}) custom-call(f32[16,16,128]{2,1,0:T(8,128)S(1)} %all-to-all-done.theta_ref, bf16[512,2048]{1,0:T(8,128)(2,1)S(1)} %get-tuple-element.12.low_ref, f32[8,2048]{1,0:T(8,128)S(1)} %get-tuple-element.13.high_ref, f32[64,2048]{1,0:T(8,128)S(1)} %get-tuple-element.14.x_ref), custom_call_target="tpu_custom_call" | custom-call | tf_op jit(solution)/shard_map/field/pallas_call | solution.py:272
  28.6 0.1 broadcast_in_dim.2
  28.7 15.1 %all_to_all.15.parts_ref = f32[32,8,512]{2,1,0:T(8,128)S(1)} all-to-all(f32[32,8,512]{2,1,0:T(8,128)S(1)} %broadcast_in_dim.2), channel_id=1, replica_groups={{21,22,23,24,25,26,27,28,29,30,31,0,1,2,3,4,5,6,7,8,9,10,11,12,13,14,15..., dimensions={0} | all-to-all | bytes 1048576 | tf_op jit(solution)/shard_map/all_to_all | solution.py:282
  43.8 1.8 %gradient.1 = (f32[2,2048]{1,0:T(2,128)}, f32[16,16,128]{2,1,0:T(8,128)S(1)}) custom-call(f32[32,8,512]{2,1,0:T(8,128)S(1)} %all_to_all.15.parts_ref, f32[8,512]{1,0:T(8,128)S(1)} %reshape.23.direct_ref, f32[4,512]{1,0:T(4,128)S(1)} %reshape.24.noise_ref, s32[4,512]{1,0:T(4,128)S(1)} %reshape.20.prow_ref, s32[4,512]{1,0:T(4,128)S(1)} %reshape.21.pcol_ref, ...), custom_call_target="tpu_custom_call" | custom-call | tf_op jit(solution)/shard_map/gradient/pallas_call | solution.py:283
  45.6 19.0 %all_to_all.16 = f32[16,16,128]{2,1,0:T(8,128)S(1)} all-to-all(f32[16,16,128]{2,1,0:T(8,128)S(1)} %get-tuple-element.20), channel_id=1, replica_groups={{320,352,384,416,448,480,0,32,64,96,128,160,192,224,256,288},{321,353,3..., dimensions={0} | all-to-all | bytes 262144 | tf_op jit(solution)/shard_map/all_to_all | solution.py:299
  64.6 0.1 fusion
  64.7 0.6 pad_maximum_fusion
  (1 shorter events, 0.0 us)
Async XLA Ops:
  0.6 0.7 %copy-start = (f32[32,64]{1,0:T(8,128)S(1)}, f32[32,64]{1,0:T(8,128)}, u32[]{:S(2)}) copy-start(f32[32,64]{1,0:T(8,128)} %theta_ref.1) | copy-start | bytes 24580
  2.1 25.3 %all-to-all-start = ((f32[16,16,128]{2,1,0:T(8,128)}), f32[16,16,128]{2,1,0:T(8,128)S(1)}, u32[]{:S(2)}, u32[]{:S(2)}) async-start(f32[16,16,128]{2,1,0:T(8,128)} %pack.1), calls=%async_computation | async-start | bytes 262144 | tf_op jit(solution)/shard_map/all_to_all | solution.py:257

commit v3 on v2

--- a/solution.py
+++ b/solution.py
@@ -97,11 +97,17 @@
     return out
 
 
-def pack_kernel(theta_ref, out_ref):
-    v = theta_ref[...]
+def pack_kernel(theta_ref, out_ref, in_ref, held_ref, sems):
+    fetch = pltpu.make_async_copy(theta_ref, in_ref, sems.at[0])
+    fetch.start()
+    fetch.wait()
+    v = in_ref[...]
     v = jnp.concatenate([v[:16], v[16:]], 1)
     for z in range(out_ref.shape[0]):
-        out_ref[z] = v
+        held_ref[z] = v
+    store = pltpu.make_async_copy(held_ref, out_ref, sems.at[1])
+    store.start()
+    store.wait()
 
 
 def table_kernel(prow_ref, pcol_ref, rows_ref, low_ref, high_ref, x_ref):
@@ -175,7 +181,7 @@
 
 
 def gradient_kernel(
-    parts_ref, direct_ref, noise_ref, prow_ref, pcol_ref, low_ref, high_ref, x_ref, u_ref, field_ref, out_ref, held_ref, whi_ref, wlo_ref, sem
+    parts_ref, direct_ref, noise_ref, prow_ref, pcol_ref, low_ref, high_ref, x_ref, u_ref, field_ref, out_ref, held_ref, w_ref, sem
 ):
     _, _, scale = slopes(prow_ref, pcol_ref)
     total = jnp.sum(parts_ref[...], 0)
@@ -201,16 +207,13 @@
         w = jnp.concatenate([w_re, w_im], 0)
         for g in range(2):
             hi, lo = split(w * high_ref[g : g + 1, cols])
-            whi_ref[128 * g : 128 * g + 64, cols] = hi
-            wlo_ref[128 * g : 128 * g + 64, cols] = lo
+            w_ref[128 * g : 128 * g + 64, cols] = hi
+            w_ref[256 + 128 * g : 320 + 128 * g, cols] = lo
             hi, lo = split(w * high_ref[4 + g : 5 + g, cols])
-            whi_ref[128 * g + 64 : 128 * g + 128, cols] = hi
-            wlo_ref[128 * g + 64 : 128 * g + 128, cols] = lo
-    sums = (
-        mm_nt(whi_ref[...], low_ref[0 : 2 * LOW])
-        + mm_nt(wlo_ref[...], low_ref[0 : 2 * LOW])
-        + mm_nt(whi_ref[...], low_ref[2 * LOW :])
-    )
+            w_ref[128 * g + 64 : 128 * g + 128, cols] = hi
+            w_ref[320 + 128 * g : 384 + 128 * g, cols] = lo
+    first = mm_nt(w_ref[...], low_ref[0 : 2 * LOW])
+    sums = first[:256] + first[256:] + mm_nt(w_ref[0:256], low_ref[2 * LOW :])
     blocks = [None] * 8
     for g in range(2):
         v = sums[128 * g : 128 * g + 128]
@@ -248,12 +251,19 @@
     sent = pl.pallas_call(
         pack_kernel,
         out_shape=jax.ShapeDtypeStruct((peers, 16, 128), F32),
+        in_specs=[pl.BlockSpec(memory_space=pltpu.HBM)],
+        out_specs=pl.BlockSpec(memory_space=pltpu.HBM),
+        scratch_shapes=[
+            pltpu.VMEM(theta.shape, F32),
+            pltpu.VMEM((peers, 16, 128), F32),
+            pltpu.SemaphoreType.DMA((2,)),
+        ],
         compiler_params=params,
         name="pack",
     )(theta)
     along_in = [[(i + TURN_IN) % peers for i in range(peers)]]
     along_out = [[(i + TURN_OUT) % peers for i in range(peers)]]
-    plane = [[(i + 21) % elems for i in range(elems)]]
+    plane = [[(2 * i + 20) % elems + core for i in range(elems // 2)] for core in (0, 1)]
     angles = lax.all_to_all(sent, "pts", 0, 0, axis_index_groups=along_in, tiled=True)
     prow = point_rows.reshape(CHUNKS, CW)
     pcol = point_cols.reshape(CHUNKS, CW)
@@ -279,7 +289,8 @@
         name="field",
     )(angles, low, high, beam)
     part, direct, noise = lax.optimization_barrier((part, direct, noise))
-    parts = lax.all_to_all(jnp.broadcast_to(part[None], (elems, 8, CW)), "elem", 0, 0, axis_index_groups=plane, tiled=True)
+    part = part + lax.ppermute(part, "elem", [(i, i ^ 1) for i in range(elems)])
+    parts = lax.all_to_all(jnp.broadcast_to(part[None], (elems // 2, 8, CW)), "elem", 0, 0, axis_index_groups=plane, tiled=True)
     field, grads = pl.pallas_call(
         gradient_kernel,
         out_shape=(
@@ -289,8 +300,7 @@
         out_specs=(pl.BlockSpec(memory_space=pl.ANY), pl.BlockSpec(memory_space=pltpu.VMEM)),
         scratch_shapes=[
             pltpu.VMEM((2, points), F32),
-            pltpu.VMEM((256, points), BF16),
-            pltpu.VMEM((256, points), BF16),
+            pltpu.VMEM((512, points), BF16),
             pltpu.SemaphoreType.DMA,
         ],
         compiler_params=params,

time: 65.9 us -> 65.3 us (level)
  the two profiles are of different devices: /device:TPU:2 before, /device:TPU:16 now
where the time goes in v3:
time: 65.3 us; the launch traced here: 64.6 us
  blocking collectives  30.3 us (46%)
  starting transfers between devices  19 us (29%)
  Pallas kernels  6.07 us (9%)
  local copies, waits for them, and re-layouts  4.38 us (7%)
  waiting for transfers between devices  3.5 us (5%)
  between operations  0.69 us (1%)
    all_to_all x1, blocking collectives, shards(): lax.all_to_all(grads, 'pts', 0, 0, axis_index_groups=along_out, tiled=True)  18.1 us
    all_to_all x1, starting transfers between devices, shards(): lax.all_to_all(sent, 'pts', 0, 0, axis_index_groups=along_in, tiled=True)  17.1 us
    all_to_all x1, blocking collectives, shards(): lax.all_to_all(jnp.broadcast_to(part[None], (elems // 2, 8, CW)), 'elem',...  12.2 us
    all_to_all x1, waiting for transfers between devices, shards(): lax.all_to_all(sent, 'pts', 0, 0, axis_index_groups=along_in, tiled=True)  2.35 us
    pallas_call x1, Pallas kernels, shards(): pl.pallas_call(table_kernel, out_shape=(jax.ShapeDtypeStruct((4 * LOW, po...  2.27 us
    ppermute x1, starting transfers between devices, shards(): part = part + lax.ppermute(part, 'elem', [(i, i ^ 1) for i in range(elems)])  1.92 us
    pallas_call x1, Pallas kernels, shards(): pl.pallas_call(gradient_kernel, out_shape=(jax.ShapeDtypeStruct((2, point...  1.79 us
  transfers between devices with their start and end apart: 2, of which 2 were waited for; matrix products, arithmetic and copies ran while one was open for 6% of the time, Pallas kernels for 4%

profile of v3, /device:TPU:16, one launch (start us, length us, event | category | flops | bytes accessed | tf_op | source)
XLA Modules:
  0.0 64.6 jit_solution(12709633479945862400)
XLA Ops:
  0.6 0.0 copy-start
  0.6 0.7 %copy-done = f32[32,64]{1,0:T(8,128)S(1)} copy-done((f32[32,64]{1,0:T(8,128)S(1)}, f32[32,64]{1,0:T(8,128)}, u32[]{:S(2)}) %copy-start) | copy-done | bytes 8216
  1.3 0.7 %pack.1 = f32[16,16,128]{2,1,0:T(8,128)} custom-call(f32[32,64]{1,0:T(8,128)S(1)} %copy-done), custom_call_target="tpu_custom_call" | custom-call | tf_op jit(solution)/shard_map/pack/pallas_call | solution.py:251
  2.1 17.1 %all-to-all-start = ((f32[16,16,128]{2,1,0:T(8,128)}), f32[16,16,128]{2,1,0:T(8,128)S(1)}, u32[]{:S(2)}, u32[]{:S(2)}) async-start(f32[16,16,128]{2,1,0:T(8,128)} %pack.1), calls=%async_computation | async-start | bytes 262144 | tf_op jit(solution)/shard_map/all_to_all | solution.py:267
  19.2 0.7 %reshape.20.prow_ref = s32[4,512]{1,0:T(4,128)S(1)} reshape(s32[2048]{0:T(1024)} %param.8) | data formatting | bytes 16384 | tf_op jit(solution)/shard_map/reshape | solution.py:268
  19.9 0.7 %reshape.21.pcol_ref = s32[4,512]{1,0:T(4,128)S(1)} reshape(s32[2048]{0:T(1024)} %param.9) | data formatting | bytes 16384 | tf_op jit(solution)/shard_map/reshape | solution.py:269
  20.6 0.7 %reshape.24.noise_ref = f32[4,512]{1,0:T(4,128)S(1)} reshape(f32[2048]{0:T(1024)} %param.11) | data formatting | bytes 16384 | tf_op jit(solution)/shard_map/reshape | solution.py:271
  21.3 0.7 %copy.8.rows_ref = s32[32,1]{1,0:T(8,128)S(1)} copy(s32[32,1]{0,1:T(1,128)} %bitcast.1) | data formatting | bytes 256 | tf_op jit(solution)/shard_map/reshape | solution.py:281
  22.0 0.7 %reshape.23.direct_ref = f32[8,512]{1,0:T(8,128)S(1)} reshape(f32[2,2048]{1,0:T(2,128)} %param.10) | data formatting | bytes 32768 | tf_op jit(solution)/shard_map/reshape | solution.py:270
  22.8 2.3 %tables.1 = (bf16[512,2048]{1,0:T(8,128)(2,1)S(1)}, f32[8,2048]{1,0:T(8,128)S(1)}, f32[64,2048]{1,0:T(8,128)S(1)}) custom-call(s32[4,512]{1,0:T(4,128)S(1)} %reshape.20.prow_ref, s32[4,512]{1,0:T(4,128)S(1)} %reshape.21.pcol_ref, s32[32,1]{1,0:T(8,128)S(1)} %copy.8.rows_ref), custom_call_target="tpu_custom_call" | custom-call | tf_op jit(solution)/shard_map/tables/pallas_call | solution.py:272
  25.0 2.4 %all-to-all-done.theta_ref = f32[16,16,128]{2,1,0:T(8,128)S(1)} async-done(((f32[16,16,128]{2,1,0:T(8,128)}), f32[16,16,128]{2,1,0:T(8,128)S(1)}, u32[]{:S(2)}, u32[]{:S(2)}) %all-to-all-start) | async-done | bytes 131104 | tf_op jit(solution)/shard_map/all_to_all | solution.py:267
  27.4 1.3 %field.1 = (f32[8,512]{1,0:T(8,128)S(1)}, f32[64,1024]{1,0:T(8,128)S(1)}) custom-call(f32[16,16,128]{2,1,0:T(8,128)S(1)} %all-to-all-done.theta_ref, bf16[512,2048]{1,0:T(8,128)(2,1)S(1)} %get-tuple-element.12.low_ref, f32[8,2048]{1,0:T(8,128)S(1)} %get-tuple-element.13.high_ref, f32[64,2048]{1,0:T(8,128)S(1)} %get-tuple-element.14.x_ref), custom_call_target="tpu_custom_call" | custom-call | tf_op jit(solution)/shard_map/field/pallas_call | solution.py:282
  28.7 1.9 %collective-permute-start = (f32[8,512]{1,0:T(8,128)S(1)}, f32[8,512]{1,0:T(8,128)S(1)}, u32[]{:S(2)}, u32[]{:S(2)}) collective-permute-start(f32[8,512]{1,0:T(8,128)S(1)} %get-tuple-element.16), channel_id=1, source_target_pairs={{0,1},{1,0},{2,3},{3,2},{4,5},{5,4},{6,7},{7,6},{8,9},{9,8},{10,11... | collective-permute-start | bytes 49160 | tf_op jit(solution)/shard_map/ppermute | solution.py:292
  30.6 1.1 %collective-permute-done = f32[8,512]{1,0:T(8,128)S(1)} collective-permute-done((f32[8,512]{1,0:T(8,128)S(1)}, f32[8,512]{1,0:T(8,128)S(1)}, u32[]{:S(2)}, u32[]{:S(2)}) %collective-permute-start) | collective-permute-done | bytes 16416 | tf_op jit(solution)/shard_map/ppermute | solution.py:292
  31.8 12.2 %all_to_all.15.parts_ref = f32[16,8,512]{2,1,0:T(8,128)S(1)} all-to-all(f32[16,8,512]{2,1,0:T(8,128)S(1)} %broadcast_in_dim.2), channel_id=1, replica_groups={{20,22,24,26,28,30,0,2,4,6,8,10,12,14,16,18},{21,23,25,27,29,31,1,3,5,7..., dimensions={0} | all-to-all | bytes 524288 | tf_op jit(solution)/shard_map/all_to_all | solution.py:293
  44.0 1.8 %gradient.1 = (f32[2,2048]{1,0:T(2,128)}, f32[16,16,128]{2,1,0:T(8,128)S(1)}) custom-call(f32[16,8,512]{2,1,0:T(8,128)S(1)} %all_to_all.15.parts_ref, f32[8,512]{1,0:T(8,128)S(1)} %reshape.23.direct_ref, f32[4,512]{1,0:T(4,128)S(1)} %reshape.24.noise_ref, s32[4,512]{1,0:T(4,128)S(1)} %reshape.20.prow_ref, s32[4,512]{1,0:T(4,128)S(1)} %reshape.21.pcol_ref, ...), custom_call_target="tpu_custom_call" | custom-call | tf_op jit(solution)/shard_map/gradient/pallas_call | solution.py:294
  45.8 18.1 %all_to_all.16 = f32[16,16,128]{2,1,0:T(8,128)S(1)} all-to-all(f32[16,16,128]{2,1,0:T(8,128)S(1)} %get-tuple-element.20), channel_id=1, replica_groups={{320,352,384,416,448,480,0,32,64,96,128,160,192,224,256,288},{321,353,3..., dimensions={0} | all-to-all | bytes 262144 | tf_op jit(solution)/shard_map/all_to_all | solution.py:309
  63.9 0.1 fusion
  64.0 0.6 pad_maximum_fusion
  (3 shorter events, 0.0 us)
Async XLA Ops:
  0.6 0.7 %copy-start = (f32[32,64]{1,0:T(8,128)S(1)}, f32[32,64]{1,0:T(8,128)}, u32[]{:S(2)}) copy-start(f32[32,64]{1,0:T(8,128)} %theta_ref.1) | copy-start | bytes 24580
  2.1 25.3 %all-to-all-start = ((f32[16,16,128]{2,1,0:T(8,128)}), f32[16,16,128]{2,1,0:T(8,128)S(1)}, u32[]{:S(2)}, u32[]{:S(2)}) async-start(f32[16,16,128]{2,1,0:T(8,128)} %pack.1), calls=%async_computation | async-start | bytes 262144 | tf_op jit(solution)/shard_map/all_to_all | solution.py:267
  28.7 3.1 %collective-permute-start = (f32[8,512]{1,0:T(8,128)S(1)}, f32[8,512]{1,0:T(8,128)S(1)}, u32[]{:S(2)}, u32[]{:S(2)}) collective-permute-start(f32[8,512]{1,0:T(8,128)S(1)} %get-tuple-element.16), channel_id=1, source_target_pairs={{0,1},{1,0},{2,3},{3,2},{4,5},{5,4},{6,7},{7,6},{8,9},{9,8},{10,11... | collective-permute-start | bytes 49160 | tf_op jit(solution)/shard_map/ppermute | solution.py:292

commit v4 on v3

--- a/solution.py
+++ b/solution.py
@@ -181,18 +181,14 @@
 
 
 def gradient_kernel(
-    parts_ref, direct_ref, noise_ref, prow_ref, pcol_ref, low_ref, high_ref, x_ref, u_ref, field_ref, out_ref, held_ref, w_ref, sem
+    parts_ref, direct_ref, noise_ref, prow_ref, pcol_ref, low_ref, high_ref, x_ref, u_ref, field_ref, out_ref, w_ref
 ):
     _, _, scale = slopes(prow_ref, pcol_ref)
     total = jnp.sum(parts_ref[...], 0)
     re = direct_ref[0:4] + scale * total[0:4]
     im = direct_ref[4:8] + scale * total[4:8]
-    for r in range(CHUNKS):
-        cols = slice(CW * r, CW * r + CW)
-        held_ref[0:1, cols] = re[r : r + 1]
-        held_ref[1:2, cols] = im[r : r + 1]
-    copy = pltpu.make_async_copy(held_ref, field_ref, sem)
-    copy.start()
+    field_ref[0:4] = re
+    field_ref[4:8] = im
     power = noise_ref[...] + re * re + im * im
     q_re = re * scale / power
     q_im = -im * scale / power
@@ -240,7 +236,16 @@
         d = blocks[n] if n % 2 else back[16 * n : 16 * n + 32]
         out_ref[(2 * n - TURN_OUT) % 16] = jnp.concatenate([d[:16, :64], d[16:, :64]], 1)
         out_ref[(2 * n + 1 - TURN_OUT) % 16] = jnp.concatenate([d[:16, 64:], d[16:, 64:]], 1)
-    copy.wait()
+
+
+def last_kernel(got_ref, held_ref, grad_ref, field_ref):
+    total = jnp.sum(got_ref[...], 0)
+    grad_ref[0:16] = total[:, :64]
+    grad_ref[16:32] = total[:, 64:]
+    for r in range(CHUNKS):
+        cols = slice(CW * r, CW * r + CW)
+        field_ref[0:1, cols] = held_ref[r : r + 1]
+        field_ref[1:2, cols] = held_ref[r + 4 : r + 5]
 
 
 def shards(theta, panel_rows, point_rows, point_cols, direct, noise):
@@ -294,21 +299,23 @@
     field, grads = pl.pallas_call(
         gradient_kernel,
         out_shape=(
-            jax.ShapeDtypeStruct((2, points), F32),
+            jax.ShapeDtypeStruct((8, CW), F32),
             jax.ShapeDtypeStruct((peers, 16, 128), F32),
         ),
-        out_specs=(pl.BlockSpec(memory_space=pl.ANY), pl.BlockSpec(memory_space=pltpu.VMEM)),
-        scratch_shapes=[
-            pltpu.VMEM((2, points), F32),
-            pltpu.VMEM((512, points), BF16),
-            pltpu.SemaphoreType.DMA,
-        ],
+        scratch_shapes=[pltpu.VMEM((512, points), BF16)],
         compiler_params=params,
         name="gradient",
     )(parts, direct, noise, prow, pcol, low, high, beam, phasors)
-    total = jnp.sum(lax.all_to_all(grads, "pts", 0, 0, axis_index_groups=along_out, tiled=True), 0)
-    grad = jnp.concatenate([total[:, :64], total[:, 64:]], 0)
-    return grad, field
+    got = lax.all_to_all(grads, "pts", 0, 0, axis_index_groups=along_out, tiled=True)
+    return pl.pallas_call(
+        last_kernel,
+        out_shape=(
+            jax.ShapeDtypeStruct(theta.shape, F32),
+            jax.ShapeDtypeStruct((2, points), F32),
+        ),
+        compiler_params=params,
+        name="last",
+    )(got, field)
 
 
 def solution(mesh):

time: 65.3 us -> 64.7 us (level)
    pallas_call x1 -> x2, Pallas kernels: 1.79 us -> 1.93 us  [the longest x1 1.24 us: shards(): pl.pallas_call(gradient_kernel, out_shape=(jax.ShapeDtypeStruct((8, CW),...]
where the time goes in v4:
time: 64.7 us; the launch traced here: 64 us
  blocking collectives  30.3 us (47%)
  starting transfers between devices  19 us (29%)
  Pallas kernels  6.22 us (10%)
  local copies, waits for them, and re-layouts  4.31 us (7%)
  waiting for transfers between devices  3.5 us (5%)
  between operations  0.68 us (1%)
    all_to_all x1, blocking collectives, shards(): lax.all_to_all(grads, 'pts', 0, 0, axis_index_groups=along_out, tiled=True)  18.1 us
    all_to_all x1, starting transfers between devices, shards(): lax.all_to_all(sent, 'pts', 0, 0, axis_index_groups=along_in, tiled=True)  17.1 us
    all_to_all x1, blocking collectives, shards(): lax.all_to_all(jnp.broadcast_to(part[None], (elems // 2, 8, CW)), 'elem',...  12.2 us
    all_to_all x1, waiting for transfers between devices, shards(): lax.all_to_all(sent, 'pts', 0, 0, axis_index_groups=along_in, tiled=True)  2.35 us
    pallas_call x1, Pallas kernels, shards(): pl.pallas_call(table_kernel, out_shape=(jax.ShapeDtypeStruct((4 * LOW, po...  2.27 us
    ppermute x1, starting transfers between devices, shards(): part = part + lax.ppermute(part, 'elem', [(i, i ^ 1) for i in range(elems)])  1.92 us
  transfers between devices with their start and end apart: 2, of which 2 were waited for; matrix products, arithmetic and copies ran while one was open for 6% of the time, Pallas kernels for 4%

profile of v4, /device:TPU:16, one launch (start us, length us, event | category | flops | bytes accessed | tf_op | source)
XLA Modules:
  0.0 64.0 jit_solution(6299702892961516070)
XLA Ops:
  0.6 0.0 copy-start
  0.6 0.7 %copy-done = f32[32,64]{1,0:T(8,128)S(1)} copy-done((f32[32,64]{1,0:T(8,128)S(1)}, f32[32,64]{1,0:T(8,128)}, u32[]{:S(2)}) %copy-start) | copy-done | bytes 8216
  1.3 0.7 %pack.1 = f32[16,16,128]{2,1,0:T(8,128)} custom-call(f32[32,64]{1,0:T(8,128)S(1)} %copy-done), custom_call_target="tpu_custom_call" | custom-call | tf_op jit(solution)/shard_map/pack/pallas_call | solution.py:256
  2.1 17.1 %all-to-all-start = ((f32[16,16,128]{2,1,0:T(8,128)}), f32[16,16,128]{2,1,0:T(8,128)S(1)}, u32[]{:S(2)}, u32[]{:S(2)}) async-start(f32[16,16,128]{2,1,0:T(8,128)} %pack.1), calls=%async_computation | async-start | bytes 262144 | tf_op jit(solution)/shard_map/all_to_all | solution.py:272
  19.2 0.7 %reshape.20.prow_ref = s32[4,512]{1,0:T(4,128)S(1)} reshape(s32[2048]{0:T(1024)} %param.8) | data formatting | bytes 16384 | tf_op jit(solution)/shard_map/reshape | solution.py:273
  19.9 0.7 %reshape.21.pcol_ref = s32[4,512]{1,0:T(4,128)S(1)} reshape(s32[2048]{0:T(1024)} %param.9) | data formatting | bytes 16384 | tf_op jit(solution)/shard_map/reshape | solution.py:274
  20.6 0.7 %reshape.24.noise_ref = f32[4,512]{1,0:T(4,128)S(1)} reshape(f32[2048]{0:T(1024)} %param.11) | data formatting | bytes 16384 | tf_op jit(solution)/shard_map/reshape | solution.py:276
  21.3 0.7 %copy.8.rows_ref = s32[32,1]{1,0:T(8,128)S(1)} copy(s32[32,1]{0,1:T(1,128)} %bitcast.1) | data formatting | bytes 256 | tf_op jit(solution)/shard_map/reshape | solution.py:286
  22.0 0.7 %reshape.23.direct_ref = f32[8,512]{1,0:T(8,128)S(1)} reshape(f32[2,2048]{1,0:T(2,128)} %param.10) | data formatting | bytes 32768 | tf_op jit(solution)/shard_map/reshape | solution.py:275
  22.8 2.3 %tables.1 = (bf16[512,2048]{1,0:T(8,128)(2,1)S(1)}, f32[8,2048]{1,0:T(8,128)S(1)}, f32[64,2048]{1,0:T(8,128)S(1)}) custom-call(s32[4,512]{1,0:T(4,128)S(1)} %reshape.20.prow_ref, s32[4,512]{1,0:T(4,128)S(1)} %reshape.21.pcol_ref, s32[32,1]{1,0:T(8,128)S(1)} %copy.8.rows_ref), custom_call_target="tpu_custom_call" | custom-call | tf_op jit(solution)/shard_map/tables/pallas_call | solution.py:277
  25.0 2.4 %all-to-all-done.theta_ref = f32[16,16,128]{2,1,0:T(8,128)S(1)} async-done(((f32[16,16,128]{2,1,0:T(8,128)}), f32[16,16,128]{2,1,0:T(8,128)S(1)}, u32[]{:S(2)}, u32[]{:S(2)}) %all-to-all-start) | async-done | bytes 131104 | tf_op jit(solution)/shard_map/all_to_all | solution.py:272
  27.4 1.3 %field.1 = (f32[8,512]{1,0:T(8,128)S(1)}, f32[64,1024]{1,0:T(8,128)S(1)}) custom-call(f32[16,16,128]{2,1,0:T(8,128)S(1)} %all-to-all-done.theta_ref, bf16[512,2048]{1,0:T(8,128)(2,1)S(1)} %get-tuple-element.12.low_ref, f32[8,2048]{1,0:T(8,128)S(1)} %get-tuple-element.13.high_ref, f32[64,2048]{1,0:T(8,128)S(1)} %get-tuple-element.14.x_ref), custom_call_target="tpu_custom_call" | custom-call | tf_op jit(solution)/shard_map/field/pallas_call | solution.py:287
  28.7 1.9 %collective-permute-start = (f32[8,512]{1,0:T(8,128)S(1)}, f32[8,512]{1,0:T(8,128)S(1)}, u32[]{:S(2)}, u32[]{:S(2)}) collective-permute-start(f32[8,512]{1,0:T(8,128)S(1)} %get-tuple-element.16), channel_id=1, source_target_pairs={{0,1},{1,0},{2,3},{3,2},{4,5},{5,4},{6,7},{7,6},{8,9},{9,8},{10,11... | collective-permute-start | bytes 49160 | tf_op jit(solution)/shard_map/ppermute | solution.py:297
  30.6 1.1 %collective-permute-done = f32[8,512]{1,0:T(8,128)S(1)} collective-permute-done((f32[8,512]{1,0:T(8,128)S(1)}, f32[8,512]{1,0:T(8,128)S(1)}, u32[]{:S(2)}, u32[]{:S(2)}) %collective-permute-start) | collective-permute-done | bytes 16416 | tf_op jit(solution)/shard_map/ppermute | solution.py:297
  31.8 12.2 %all_to_all.15.parts_ref = f32[16,8,512]{2,1,0:T(8,128)S(1)} all-to-all(f32[16,8,512]{2,1,0:T(8,128)S(1)} %broadcast_in_dim.2), channel_id=1, replica_groups={{20,22,24,26,28,30,0,2,4,6,8,10,12,14,16,18},{21,23,25,27,29,31,1,3,5,7..., dimensions={0} | all-to-all | bytes 524288 | tf_op jit(solution)/shard_map/all_to_all | solution.py:298
  44.0 1.2 %gradient.1 = (f32[8,512]{1,0:T(8,128)S(1)}, f32[16,16,128]{2,1,0:T(8,128)S(1)}) custom-call(f32[16,8,512]{2,1,0:T(8,128)S(1)} %all_to_all.15.parts_ref, f32[8,512]{1,0:T(8,128)S(1)} %reshape.23.direct_ref, f32[4,512]{1,0:T(4,128)S(1)} %reshape.24.noise_ref, s32[4,512]{1,0:T(4,128)S(1)} %reshape.20.prow_ref, s32[4,512]{1,0:T(4,128)S(1)} %reshape.21.pcol_ref, ...), custom_call_target="tpu_custom_call" | custom-call | tf_op jit(solution)/shard_map/gradient/pallas_call | solution.py:299
  45.2 18.1 %all_to_all.16.got_ref = f32[16,16,128]{2,1,0:T(8,128)S(1)} all-to-all(f32[16,16,128]{2,1,0:T(8,128)S(1)} %get-tuple-element.20), channel_id=1, replica_groups={{320,352,384,416,448,480,0,32,64,96,128,160,192,224,256,288},{321,353,3..., dimensions={0} | all-to-all | bytes 262144 | tf_op jit(solution)/shard_map/all_to_all | solution.py:309
  63.3 0.7 %last.1 = (f32[32,64]{1,0:T(8,128)}, f32[2,2048]{1,0:T(2,128)}) custom-call(f32[16,16,128]{2,1,0:T(8,128)S(1)} %all_to_all.16.got_ref, f32[8,512]{1,0:T(8,128)S(1)} %get-tuple-element.21.held_ref), custom_call_target="tpu_custom_call" | custom-call | tf_op jit(solution)/shard_map/last/pallas_call | solution.py:310
  (2 shorter events, 0.0 us)
Async XLA Ops:
  0.6 0.7 %copy-start = (f32[32,64]{1,0:T(8,128)S(1)}, f32[32,64]{1,0:T(8,128)}, u32[]{:S(2)}) copy-start(f32[32,64]{1,0:T(8,128)} %theta_ref.1) | copy-start | bytes 24580
  2.1 25.3 %all-to-all-start = ((f32[16,16,128]{2,1,0:T(8,128)}), f32[16,16,128]{2,1,0:T(8,128)S(1)}, u32[]{:S(2)}, u32[]{:S(2)}) async-start(f32[16,16,128]{2,1,0:T(8,128)} %pack.1), calls=%async_computation | async-start | bytes 262144 | tf_op jit(solution)/shard_map/all_to_all | solution.py:272
  28.7 3.1 %collective-permute-start = (f32[8,512]{1,0:T(8,128)S(1)}, f32[8,512]{1,0:T(8,128)S(1)}, u32[]{:S(2)}, u32[]{:S(2)}) collective-permute-start(f32[8,512]{1,0:T(8,128)S(1)} %get-tuple-element.16), channel_id=1, source_target_pairs={{0,1},{1,0},{2,3},{3,2},{4,5},{5,4},{6,7},{7,6},{8,9},{9,8},{10,11... | collective-permute-start | bytes 49160 | tf_op jit(solution)/shard_map/ppermute | solution.py:297
